TPU v7x, 256 devices: a whole 4x4x8 slice. The times are simulated.
256 devices in a mesh: grp: 32 (over y, x, core), ctx: 8 (over z).
Axes of the slice: x: 4, y: 4, z: 8, core: 2. Of those that a mesh axis runs over, the one named last changes fastest.
Arguments:
- hidden: bfloat16 [65536, 3584], P(('grp', 'ctx')), may hold values from -6 to 6
- norm_gain: float32 [3584], replicated, may hold values from 0.1 to 1.9
- qkv_weight: bfloat16 [3584, 2304], P('grp'), may hold values from -4.008919 to 4.008919
- qkv_bias: float32 [2304], replicated, may hold values from -3 to 3
- repo_lengths: int32 [32, 6], P('grp'), may hold values from 1 to 1024, 2048 in all within a row
Outputs:
- context: bfloat16 [65536, 1792], P(('grp', 'ctx'))
All inputs are finite; a program needn't handle non-finite values.
Results may differ from a plain program's by a relative error of at most 0.0059.
The roundings to bfloat16 on the way count: a program that leaves them out, or rounds other values in their place, can miss the bound.
Values may be sent and summed in bfloat16 or wider, within the bound.
No kernel may reach another device: no remote copies, remote signals or barrier semaphores. Data moves between devices by JAX's collectives and lax.ppermute only.
A program may use at most 128 MiB of HBM per device.

v0:
```python
import jax
import jax.numpy as jnp
from jax import lax
from jax.sharding import PartitionSpec as P

HEAD_DIM = 128
HEADS = 14
KV_HEADS = 2
rope_base = 1000000.0
norm_eps = 1e-06


def rope_tables(position):
    inv_freq = rope_base ** (-jnp.arange(0, HEAD_DIM, 2, dtype=jnp.float32) / HEAD_DIM)
    angle = position.astype(jnp.float32)[:, None] * inv_freq[None, :]
    angle = jnp.concatenate([angle, angle], axis=-1)
    return (jnp.cos(angle), jnp.sin(angle))


def rotate(values, cosine, sine_part):
    half = HEAD_DIM // 2
    first = values[..., :half]
    second = values[..., half:]
    turned = jnp.concatenate([-second, first], axis=-1)
    return values * cosine[:, None, :] + turned * sine_part[:, None, :]


def body(hidden, norm_gain, qkv_weight, qkv_bias, repo_lengths):
    tok_rows = hidden.shape[0]
    group_heads = HEADS // KV_HEADS
    hidden_f32 = hidden.astype(jnp.float32)
    normed = (
        hidden_f32
        * lax.rsqrt(jnp.mean(hidden_f32 * hidden_f32, axis=1, keepdims=True) + norm_eps)
        * norm_gain[None, :]
    ).astype(jnp.bfloat16)
    projected_f32 = jnp.dot(
        normed,
        lax.all_gather(qkv_weight, "grp", axis=0, tiled=True),
        preferred_element_type=jnp.float32,
    )
    projected = (projected_f32 + qkv_bias[None, :]).astype(jnp.bfloat16)
    lengths = repo_lengths[0]
    tok_index = lax.axis_index("ctx") * tok_rows + jnp.arange(tok_rows, dtype=jnp.int32)
    repo_ends = jnp.cumsum(lengths)
    repo_start = jnp.sum(
        jnp.where(tok_index[:, None] >= repo_ends[None, :], lengths[None, :], 0), axis=1
    )
    cosine, sine_part = rope_tables(tok_index - repo_start)
    q_cols = HEADS * HEAD_DIM
    k_cols = KV_HEADS * HEAD_DIM
    query_f32 = projected[:, :q_cols].astype(jnp.float32).reshape(tok_rows, HEADS, HEAD_DIM)
    key_f32 = (
        projected[:, q_cols : q_cols + k_cols]
        .astype(jnp.float32)
        .reshape(tok_rows, KV_HEADS, HEAD_DIM)
    )
    queries = (
        rotate(query_f32, cosine, sine_part)
        .astype(jnp.bfloat16)
        .reshape(tok_rows, KV_HEADS, group_heads, HEAD_DIM)
    )
    keys = rotate(key_f32, cosine, sine_part).astype(jnp.bfloat16).reshape(tok_rows, k_cols)
    values = projected[:, q_cols + k_cols :]
    row_max = jnp.full((KV_HEADS, group_heads, tok_rows), -1e30, jnp.float32)
    key_piece = lax.all_gather(keys, "ctx", axis=0, tiled=True)
    value_piece = lax.all_gather(values, "ctx", axis=0, tiled=True)
    key_count = key_piece.shape[0]
    key_heads = key_piece.reshape(key_count, KV_HEADS, HEAD_DIM)
    value_heads = value_piece.reshape(key_count, KV_HEADS, HEAD_DIM)
    scores = jnp.einsum(
        "rgho,kgo->ghrk", queries, key_heads, preferred_element_type=jnp.float32
    ) * HEAD_DIM ** (-0.5)
    key_index = jnp.arange(key_count, dtype=jnp.int32)
    allowed = (key_index[None, :] <= tok_index[:, None]) & (
        key_index[None, :] >= repo_start[:, None]
    )
    scores = jnp.where(allowed, scores, -1e30)
    new_max = jnp.maximum(row_max, jnp.max(scores, axis=-1))
    weights = jnp.where(allowed, jnp.exp(scores - new_max[..., None]), 0.0)
    new_total = jnp.sum(weights, axis=-1)
    rounded_weights = weights.astype(jnp.bfloat16)
    new_weighted = jnp.einsum(
        "ghrk,kgo->ghro", rounded_weights, value_heads, preferred_element_type=jnp.float32
    )
    result = new_weighted / new_total[..., None]
    return (
        jnp.transpose(result, (2, 0, 1, 3)).reshape(tok_rows, HEADS * HEAD_DIM).astype(jnp.bfloat16)
    )


def solution(mesh):
    in_specs = (P(("grp", "ctx"), None), P(), P("grp", None), P(), P("grp", None))
    out_specs = P(("grp", "ctx"), None)
    return jax.shard_map(body, mesh=mesh, in_specs=in_specs, out_specs=out_specs, check_vma=False)
```

profile of v0, /device:TPU:2, one launch (start us, length us, event | category | flops | bytes accessed | tf_op | source)
XLA Modules:
  0.0 203.0 jit_solution(906771220540744256)
XLA Ops:
  6.5 0.7 all-gather.4.cloned.1.call-update
  7.3 0.8 reduce-window.8
  8.2 0.7 select_reduce_fusion
  9.0 0.5 fusion.26
  9.7 1.9 fusion.7
  11.6 78.2 %all-gather.4.cloned.1.call-done = bf16[3584,2304]{1,0:T(8,128)(2,1)} async-done(((bf16[112,2304]{1,0:T(8,128)(2,1)}), bf16[3584,2304]{1,0:T(8,128)(2,1)}) %all-gather.4.cloned.1.call-update) | async-done | bytes 16515088 | tf_op jit(solution)/shard_map/all_gather | solution.py:39
  89.8 10.7 %fusion.6 = bf16[256,2304]{1,0:T(8,128)(2,1)S(1)} fusion(bf16[3584,2304]{1,0:T(8,128)(2,1)} %all-gather.4.cloned.1.call-done, bf16[256,3584]{1,0:T(8,128)(2,1)} %param.5, f32[3584]{0:T(1024)} %param.6, f32[256]{0:T(256)S(1)} %add_rsqrt_fusion, f32[2304]{0:T(1024)} %param.8), kind=kOutput, calls=%fused_computation.10 | convolution fusion | flops 4232708096 | bytes 19554304 | tf_op jit(solution)/shard_map/dot_general | solution.py:37
  100.5 0.7 slice_convert_fusion.1
  101.3 0.3 slice_negate_fusion.1
  101.7 0.4 maximum_multiply_fusion.1
  102.1 0.7 fusion.24
  102.9 0.2 all-gather.8.cloned.1.call-start
  103.1 0.5 fusion.10
  103.6 1.4 slice_convert_fusion
  105.0 1.8 copy.24
  106.8 1.1 slice_negate_fusion
  107.9 33.4 %all-gather.6.cloned.1.call-done = bf16[2048,256]{1,0:T(8,128)(2,1)} async-done(((bf16[256,256]{1,0:T(8,128)(2,1)}), bf16[2048,256]{1,0:T(8,128)(2,1)}) %all-gather.6.cloned.1.call-update) | async-done | bytes 1048592 | tf_op jit(solution)/shard_map/all_gather | solution.py:66
  141.3 2.1 %reshape.134 = bf16[2048,2,128]{2,1,0:T(2,128)(2,1)} reshape(bf16[2048,256]{1,0:T(8,128)(2,1)} %all-gather.6.cloned.1.call-done) | data formatting | bytes 2097152 | tf_op jit(solution)/shard_map/reshape | solution.py:69
  143.4 13.5 %fusion = (f32[2,7,256]{2,1,0:T(8,128)S(1)}, f32[2,2048,256,7]{2,1,3,0:T(8,128)}) fusion(pred[256,2048]{0,1:T(8,128)(4,1)S(1)} %fusion.10, f32[256,2,7,64]{0,3,2,1:T(8,128)} %bitcast.48, f32[256,2,7,64]{0,3,2,1:T(8,128)S(1)} %bitcast.47, f32[256,2,7,128]{0,3,2,1:T(8,128)S(1)} %bitcast.45, f32[256,128]{0,1:T(8,128)S(1)} %get-tuple-element.12, ...), kind=kOutput, calls=%fused_computation.2 | convolution fusion | flops 1903358464 | bytes 34879488 | tf_op jit(solution)/shard_map/rgho,kgo->ghrk/dot_general | solution.py:71
  156.9 13.5 %fusion.1 = f32[2,7,256]{2,1,0:T(8,128)S(1)} fusion(f32[2,2048,256,7]{2,1,3,0:T(8,128)} %get-tuple-element.14, f32[2,7,256]{2,1,0:T(8,128)S(1)} %broadcast_maximum_fusion, pred[256,2048]{0,1:T(8,128)(4,1)S(1)} %fusion.10), kind=kLoop, calls=%fused_computation.3 | loop fusion | flops 36696576 | bytes 29913088 | tf_op jit(solution)/shard_map/reduce_sum | solution.py:81
  170.5 9.9 %all-gather.8.cloned.1.call-done = bf16[2048,256]{1,0:T(8,128)(2,1)} async-done(((bf16[256,256]{1,0:T(8,128)(2,1)}), bf16[2048,256]{1,0:T(8,128)(2,1)}) %all-gather.8.cloned.1.call-update) | async-done | bytes 1048592 | tf_op jit(solution)/shard_map/all_gather | solution.py:67
  180.3 1.5 copy.37
  181.8 13.3 %fusion.14 = bf16[256,2,7,128]{0,3,2,1:T(8,128)(2,1)S(1)} fusion(bf16[2048,2,128,1]{0,2,3,1:T(8,128)(2,1)S(1)} %bitcast.51, f32[2,2048,256,7]{2,1,3,0:T(8,128)} %get-tuple-element.14, f32[2,7,256]{2,1,0:T(8,128)S(1)} %broadcast_maximum_fusion, pred[256,2048]{0,1:T(8,128)(4,1)S(1)} %fusion.10, f32[256,2,7]{0,2,1:T(8,128)S(1)} %bitcast.53), kind=kOutput, calls=%fused_computation.21 | convolution fusion | flops 1916665856 | bytes 31879168 | tf_op jit(solution)/shard_map/ghrk,kgo->ghro/dot_general | solution.py:83
  195.1 1.4 copy.30
  (14 shorter events, 0.6 us)
Async XLA Ops:
  6.5 83.3 %all-gather.4.cloned.1.call-start = ((), (), s32[]{:S(2)}) async-start(), calls=%async_computation | async-start | bytes 17031168 | tf_op jit(solution)/shard_map/all_gather | solution.py:39
  7.3 134.1 %all-gather.6.cloned.1.call-start = ((), (), s32[]{:S(2)}) async-start(), calls=%async_computation.1 | async-start | bytes 1179648 | tf_op jit(solution)/shard_map/all_gather | solution.py:66
  102.9 77.5 %all-gather.8.cloned.1.call-start = ((), (), s32[]{:S(2)}) async-start(), calls=%async_computation.2 | async-start | bytes 1179648 | tf_op jit(solution)/shard_map/all_gather | solution.py:67
Sparse Core Ops, SparseCore 0:
  9.9 79.8 all-gather.3
  103.0 38.2 all-gather.5
  143.1 37.1 all-gather.7
where the time goes:
time: 203 us
  waiting for transfers between devices  122 us (60%)
  matrix products  37.5 us (18%)
  other arithmetic  22.6 us (11%)
  between operations  13.2 us (7%)
  local copies, waits for them, and re-layouts  7.21 us (4%)
    all_gather x1, waiting for transfers between devices, body(): lax.all_gather(qkv_weight, 'grp', axis=0, tiled=True)  78.2 us
    all_gather x1, waiting for transfers between devices, body(): key_piece = lax.all_gather(keys, 'ctx', axis=0, tiled=True)  33.4 us
    reduce_sum x1, other arithmetic, body(): new_total = jnp.sum(weights, axis=-1)  13.5 us
    dot_general x1, matrix products, body(): jnp.einsum('rgho,kgo->ghrk', queries, key_heads, preferred_element_type=j...  13.5 us
    dot_general x1, matrix products, body(): jnp.einsum('ghrk,kgo->ghro', rounded_weights, value_heads, preferred_elem...  13.3 us
    dot_general x1, matrix products, body(): jnp.dot(normed, lax.all_gather(qkv_weight, 'grp', axis=0, tiled=True), pr...  10.7 us
    all_gather x1, waiting for transfers between devices, body(): value_piece = lax.all_gather(values, 'ctx', axis=0, tiled=True)  9.88 us
  transfers between devices with their start and end apart: 3, of which 3 were waited for; matrix products, arithmetic and copies ran while one was open for 19% of the time, Pallas kernels for 0%

commit v1 on v0

--- a/solution.py
+++ b/solution.py
@@ -63,7 +63,9 @@
     keys = rotate(key_f32, cosine, sine_part).astype(jnp.bfloat16).reshape(tok_rows, k_cols)
     values = projected[:, q_cols + k_cols :]
     row_max = jnp.full((KV_HEADS, group_heads, tok_rows), -1e30, jnp.float32)
-    key_piece = lax.all_gather(keys, "ctx", axis=0, tiled=True)
+    key_piece = jnp.concatenate(
+        lax.all_to_all(jnp.stack([keys] * lax.axis_size("ctx")), "ctx", 0, 0), axis=0
+    )
     value_piece = lax.all_gather(values, "ctx", axis=0, tiled=True)
     key_count = key_piece.shape[0]
     key_heads = key_piece.reshape(key_count, KV_HEADS, HEAD_DIM)

time: 203 us -> 198 us (0.975)
  waiting for transfers between devices: 122 us -> 106 us
  starting transfers between devices: 0.26 us -> 7.23 us
  local copies, waits for them, and re-layouts: 7.21 us -> 11.3 us
    all_gather x1 -> x0, waiting for transfers between devices: 33.4 us -> none  [body(): key_piece = lax.all_gather(keys, 'ctx', axis=0, tiled=True)]
    all_to_all x0 -> x1, waiting for transfers between devices: none -> 26.7 us  [body(): lax.all_to_all(jnp.stack([keys] * lax.axis_size('ctx')), 'ctx', 0, 0)]
    all_gather x1, waiting for transfers between devices: 9.88 us -> 0.02 us  [body(): value_piece = lax.all_gather(values, 'ctx', axis=0, tiled=True)]
    all_to_all x0 -> x1, starting transfers between devices: none -> 7.01 us  [body(): lax.all_to_all(jnp.stack([keys] * lax.axis_size('ctx')), 'ctx', 0, 0)]
    another operation x0 -> x2, local copies, waits for them, and re-layouts: none -> 3.37 us  [the longest x1 2.34 us: body(): key_heads = key_piece.reshape(key_count, KV_HEADS, HEAD_DIM)]
    all_to_all x0 -> x1, local copies, waits for them, and re-layouts: none -> 2.8 us  [body(): lax.all_to_all(jnp.stack([keys] * lax.axis_size('ctx')), 'ctx', 0, 0)]
    reshape x1 -> x0, local copies, waits for them, and re-layouts: 2.14 us -> none  [body(): key_heads = key_piece.reshape(key_count, KV_HEADS, HEAD_DIM)]
  transfers between devices with their start and end apart: 3 -> 3, of which waited for: 3 -> 2; matrix products, arithmetic and copies ran while one was open for 19% -> 21% of each run, Pallas kernels for 0% -> 0%
where the time goes in v1:
time: 198 us; the launch traced here: 197 us
  waiting for transfers between devices  106 us (54%)
  matrix products  37.6 us (19%)
  other arithmetic  21.9 us (11%)
  between operations  13.5 us (7%)
  local copies, waits for them, and re-layouts  11.3 us (6%)
  starting transfers between devices  7.23 us (4%)
    all_gather x1, waiting for transfers between devices, body(): lax.all_gather(qkv_weight, 'grp', axis=0, tiled=True)  78.2 us
    all_to_all x1, waiting for transfers between devices, body(): lax.all_to_all(jnp.stack([keys] * lax.axis_size('ctx')), 'ctx', 0, 0)  26.7 us
    dot_general x1, matrix products, body(): jnp.einsum('rgho,kgo->ghrk', queries, key_heads, preferred_element_type=j...  13.6 us
    reduce_sum x1, other arithmetic, body(): new_total = jnp.sum(weights, axis=-1)  13.4 us
    dot_general x1, matrix products, body(): jnp.einsum('ghrk,kgo->ghro', rounded_weights, value_heads, preferred_elem...  13.3 us
    dot_general x1, matrix products, body(): jnp.dot(normed, lax.all_gather(qkv_weight, 'grp', axis=0, tiled=True), pr...  10.7 us
    all_to_all x1, starting transfers between devices, body(): lax.all_to_all(jnp.stack([keys] * lax.axis_size('ctx')), 'ctx', 0, 0)  7.01 us
  transfers between devices with their start and end apart: 3, of which 2 were waited for; matrix products, arithmetic and copies ran while one was open for 21% of the time, Pallas kernels for 0%

profile of v1, /device:TPU:2, one launch (start us, length us, event | category | flops | bytes accessed | tf_op | source)
XLA Modules:
  0.0 197.3 jit_solution(8051085711001062851)
XLA Ops:
  6.5 0.7 all-gather.3.cloned.1.call-update
  7.3 0.8 reduce-window.8
  8.1 0.7 select_reduce_fusion
  8.9 0.5 fusion.26
  9.6 1.9 fusion.7
  11.6 78.2 %all-gather.3.cloned.1.call-done = bf16[3584,2304]{1,0:T(8,128)(2,1)} async-done(((bf16[112,2304]{1,0:T(8,128)(2,1)}), bf16[3584,2304]{1,0:T(8,128)(2,1)}) %all-gather.3.cloned.1.call-update) | async-done | bytes 16515088 | tf_op jit(solution)/shard_map/all_gather | solution.py:39
  89.8 10.7 %fusion.6 = bf16[256,2304]{1,0:T(8,128)(2,1)S(1)} fusion(bf16[3584,2304]{1,0:T(8,128)(2,1)} %all-gather.3.cloned.1.call-done, bf16[256,3584]{1,0:T(8,128)(2,1)} %param.5, f32[3584]{0:T(1024)} %param.6, f32[256]{0:T(256)S(1)} %add_rsqrt_fusion, f32[2304]{0:T(1024)} %param.8), kind=kOutput, calls=%fused_computation.10 | convolution fusion | flops 4232708096 | bytes 19554304 | tf_op jit(solution)/shard_map/dot_general | solution.py:37
  100.5 0.7 slice_convert_fusion.1
  101.3 0.3 slice_negate_fusion.1
  101.7 0.4 maximum_multiply_fusion.1
  102.3 1.0 stack.3
  103.3 7.0 %all-to-all-start = ((bf16[8,256,256]{1,2,0:T(8,128)(2,1)}), bf16[8,256,256]{1,2,0:T(8,128)(2,1)}, u32[]{:S(2)}, u32[]{:S(2)}) async-start(bf16[8,256,256]{1,2,0:T(8,128)(2,1)} %stack.3), calls=%async_computation | async-start | bytes 2097152 | tf_op jit(solution)/shard_map/all_to_all | solution.py:67
  110.6 0.5 fusion.10
  111.1 1.4 slice_convert_fusion
  112.5 1.8 copy.37
  114.3 1.1 slice_negate_fusion
  115.4 26.7 %all-to-all-done = bf16[8,256,256]{1,2,0:T(8,128)(2,1)} async-done(((bf16[8,256,256]{1,2,0:T(8,128)(2,1)}), bf16[8,256,256]{1,2,0:T(8,128)(2,1)}, u32[]{:S(2)}, u32[]{:S(2)}) %all-to-all-start) | async-done | bytes 1048608 | tf_op jit(solution)/shard_map/all_to_all | solution.py:67
  142.1 2.8 %copy.36 = bf16[8,256,256]{1,0,2:T(8,128)(2,1)} copy(bf16[8,256,256]{1,2,0:T(8,128)(2,1)} %all-to-all-done) | data formatting | bytes 2097152 | tf_op jit(solution)/shard_map/all_to_all | solution.py:67
  144.9 2.3 %reshape_reshape.3 = bf16[2048,2,128]{0,2,1:T(8,128)(2,1)} reshape(bf16[8,256,256]{1,0,2:T(8,128)(2,1)} %copy.36) | data formatting | bytes 2097152 | tf_op jit(solution)/shard_map/reshape;reshape | solution.py:71
  147.2 13.6 %fusion = (f32[2,7,256]{2,1,0:T(8,128)S(1)}, f32[2,2048,256,7]{2,1,3,0:T(8,128)}) fusion(pred[256,2048]{0,1:T(8,128)(4,1)S(1)} %fusion.10, f32[256,2,7,64]{0,3,2,1:T(8,128)} %bitcast.55, f32[256,2,7,64]{0,3,2,1:T(8,128)S(1)} %bitcast.54, f32[256,2,7,128]{0,3,2,1:T(8,128)S(1)} %bitcast.53, f32[256,128]{0,1:T(8,128)S(1)} %get-tuple-element.12, ...), kind=kOutput, calls=%fused_computation.2 | convolution fusion | flops 1903358464 | bytes 34879488 | tf_op jit(solution)/shard_map/rgho,kgo->ghrk/dot_general | solution.py:73
  160.8 13.4 %fusion.1 = f32[2,7,256]{2,1,0:T(8,128)S(1)} fusion(f32[2,2048,256,7]{2,1,3,0:T(8,128)} %get-tuple-element.14, f32[2,7,256]{2,1,0:T(8,128)S(1)} %broadcast_maximum_fusion, pred[256,2048]{0,1:T(8,128)(4,1)S(1)} %fusion.10), kind=kLoop, calls=%fused_computation.3 | loop fusion | flops 36696576 | bytes 29913088 | tf_op jit(solution)/shard_map/reduce_sum | solution.py:83
  174.3 1.5 copy.50
  175.8 13.3 %fusion.14 = bf16[256,2,7,128]{0,3,2,1:T(8,128)(2,1)S(1)} fusion(bf16[2048,2,128,1]{0,2,3,1:T(8,128)(2,1)S(1)} %bitcast.58, f32[2,2048,256,7]{2,1,3,0:T(8,128)} %get-tuple-element.14, f32[2,7,256]{2,1,0:T(8,128)S(1)} %broadcast_maximum_fusion, pred[256,2048]{0,1:T(8,128)(4,1)S(1)} %fusion.10, f32[256,2,7]{0,2,1:T(8,128)S(1)} %bitcast.60), kind=kOutput, calls=%fused_computation.21 | convolution fusion | flops 1916665856 | bytes 31879168 | tf_op jit(solution)/shard_map/ghrk,kgo->ghro/dot_general | solution.py:85
  189.1 1.4 copy.43
  (16 shorter events, 0.9 us)
Async XLA Ops:
  6.5 83.3 %all-gather.3.cloned.1.call-start = ((), (), s32[]{:S(2)}) async-start(), calls=%async_computation.1 | async-start | bytes 17031168 | tf_op jit(solution)/shard_map/all_gather | solution.py:39
  103.3 38.8 %all-to-all-start = ((bf16[8,256,256]{1,2,0:T(8,128)(2,1)}), bf16[8,256,256]{1,2,0:T(8,128)(2,1)}, u32[]{:S(2)}, u32[]{:S(2)}) async-start(bf16[8,256,256]{1,2,0:T(8,128)(2,1)} %stack.3), calls=%async_computation | async-start | bytes 2097152 | tf_op jit(solution)/shard_map/all_to_all | solution.py:67
  110.4 63.9 %all-gather.5.cloned.1.call-start = ((), (), s32[]{:S(2)}) async-start(), calls=%async_computation.2 | async-start | bytes 1179648 | tf_op jit(solution)/shard_map/all_gather | solution.py:69
Sparse Core Ops, SparseCore 0:
  9.9 79.8 all-gather.2
  114.4 42.5 all-gather.4
